TPU v7x, 32 devices: a whole 2x2x4 slice. The times are simulated.
32 devices in a mesh: seq: 32 (over z, y, x, core).
Axes of the slice: x: 2, y: 2, z: 4, core: 2. Of those that a mesh axis runs over, the one named last changes fastest.
Arguments:
- tokens: bfloat16 [4, 2048, 768], P(None, 'seq'), may hold values from -6 to 6
- doc_lengths: int32 [4, 16], replicated, may hold values from 1 to 512, 2048 in all within a row
- first_gain: float32 [768], replicated, may hold values from 0.5 to 1.5
- first_shift: float32 [768], replicated, may hold values from -1.75 to 1.75
- input_weight: bfloat16 [768, 2304], replicated, may hold values from -0.21875 to 0.21875
- input_bias: float32 [2304], replicated, may hold values from -1.75 to 1.75
- short_kernel: float32 [3, 2304], replicated, may hold values from -3.5 to 3.5
- short_bias: float32 [2304], replicated, may hold values from -1.75 to 1.75
- embed_weight: float32 [33, 64], replicated, may hold values from -2 to 2
- embed_bias: float32 [64], replicated, may hold values from -3.140625 to 3.140625
- inner_weight: float32 [64, 64], replicated, may hold values from -1.5 to 1.5
- inner_bias: float32 [64], replicated, may hold values from -3.140625 to 3.140625
- filter_weight: float32 [64, 768], replicated, may hold values from -0.03125 to 0.03125
- decay_rates: float32 [768], replicated, may hold values from 3.07 to 15.35
- filter_bias: float32 [768], replicated, may hold values from -3 to 3
- output_weight: bfloat16 [768, 768], replicated, may hold values from -0.21875 to 0.21875
- output_bias: float32 [768], replicated, may hold values from -1.75 to 1.75
- second_gain: float32 [768], replicated, may hold values from 0.5 to 1.5
- second_shift: float32 [768], replicated, may hold values from -1.75 to 1.75
- up_weight: bfloat16 [768, 3072], replicated, may hold values from -0.21875 to 0.21875
- up_bias: float32 [3072], replicated, may hold values from -1.75 to 1.75
- down_weight: bfloat16 [3072, 768], replicated, may hold values from -0.109375 to 0.109375
- down_bias: float32 [768], replicated, may hold values from -1.75 to 1.75
- cotangent: bfloat16 [4, 2048, 768], P(None, 'seq'), may hold values from -6 to 6
Outputs:
- output: bfloat16 [4, 2048, 768], P(None, 'seq')
- grad_tokens: bfloat16 [4, 2048, 768], P(None, 'seq')
- grad_first_gain: float32 [768], replicated
- grad_first_shift: float32 [768], replicated
- grad_input_weight: float32 [768, 2304], replicated
- grad_input_bias: float32 [2304], replicated
- grad_short_kernel: float32 [3, 2304], replicated
- grad_short_bias: float32 [2304], replicated
- grad_embed_weight: float32 [33, 64], replicated
- grad_embed_bias: float32 [64], replicated
- grad_inner_weight: float32 [64, 64], replicated
- grad_inner_bias: float32 [64], replicated
- grad_filter_weight: float32 [64, 768], replicated
- grad_decay_rates: float32 [768], replicated
- grad_filter_bias: float32 [768], replicated
- grad_output_weight: float32 [768, 768], replicated
- grad_output_bias: float32 [768], replicated
- grad_second_gain: float32 [768], replicated
- grad_second_shift: float32 [768], replicated
- grad_up_weight: float32 [768, 3072], replicated
- grad_up_bias: float32 [3072], replicated
- grad_down_weight: float32 [3072, 768], replicated
- grad_down_bias: float32 [768], replicated
Inputs may be any that keep to these rules, and one draw needn't show every extreme that they name: `doc_lengths`: the lengths of one sequence add up to 2048, and the longest document of each sequence has exactly 512 positions.
All inputs are finite; a program needn't handle non-finite values.
Results may differ from a plain program's by a relative error of at most 0.014.
Values may be sent and summed in bfloat16 or wider, within the bound.
A program may use at most 192 MiB of HBM per device.

v0:
```python
import functools
import math

import jax
import jax.numpy as jnp
from jax import lax
from jax.experimental import pallas as pl
from jax.experimental.pallas import tpu as pltpu
from jax.sharding import PartitionSpec as P

MESH = pl.DeviceIdType.MESH
EPSILON = 1e-05


def bit_of(me, bit):
    return lax.rem(lax.div(me, bit), 2)

def partner_of(me, bit):
    return me + bit - 2 * bit * bit_of(me, bit)

def halving_plan(rows, columns, order, row_unit, column_unit=128):
    steps = []
    for bit in order:
        if rows % (2 * row_unit) == 0:
            rows //= 2
            steps.append((bit, "row", rows, columns))
        elif columns % (2 * column_unit) == 0:
            columns //= 2
            steps.append((bit, "column", rows, columns))
        else:
            steps.append((bit, "full", rows, columns))
    return steps

class Reduction:
    def __init__(self, array, plan, inbox, sends, arrivals, free, me):
        self.array, self.plan, self.inbox = array, plan, inbox
        self.sends, self.arrivals, self.free, self.me = sends, arrivals, free, me
        self.row, self.column = 0, 0
        self.origin = []
        for bit, kind, rows, columns in plan:
            mine = bit_of(me, bit)
            keep, give = (self.row, self.column), (self.row, self.column)
            if kind == "row":
                keep = (self.row + mine * rows, self.column)
                give = (self.row + (1 - mine) * rows, self.column)
            elif kind == "column":
                keep = (self.row, self.column + mine * columns)
                give = (self.row, self.column + (1 - mine) * columns)
            self.origin.append((keep, give))
            self.row, self.column = keep
        self.unit_rows = plan[-1][2]
        self.unit_columns = plan[-1][3]
        self.unit_columns = min(p[3] for p in plan)
        self.unit_rows = min(p[2] for p in plan)

    def window(self, ref, origin, rows, columns):
        row, column = origin
        if not isinstance(row, int):
            row = pl.multiple_of(row, self.unit_rows)
        if not isinstance(column, int):
            column = pl.multiple_of(column, self.unit_columns)
        return ref.at[pl.ds(row, rows), pl.ds(column, columns)]

    def give_copy(self, s):
        bit, kind, rows, columns = self.plan[s]
        return pltpu.make_async_remote_copy(
            src_ref=self.window(self.array, self.origin[s][1], rows, columns),
            dst_ref=self.inbox[s],
            send_sem=self.sends.at[s], recv_sem=self.arrivals.at[s],
            device_id=(partner_of(self.me, bit),), device_id_type=MESH)

    def share_copy(self, s):
        bit, kind, rows, columns = self.plan[s]
        here = self.window(self.array, self.origin[s][0], rows, columns)
        n = len(self.plan)
        return pltpu.make_async_remote_copy(
            src_ref=here, dst_ref=here,
            send_sem=self.sends.at[n + s], recv_sem=self.arrivals.at[n + s],
            device_id=(partner_of(self.me, bit),), device_id_type=MESH)

    def give(self, s):
        self.give_copy(s).start()

    def take(self, s):
        self.give_copy(s).wait()
        bit, kind, rows, columns = self.plan[s]
        if kind != "full":
            pl.semaphore_signal(
                self.free.at[s], inc=1, device_id=(partner_of(self.me, bit),), device_id_type=MESH
            )
        row, column = self.origin[s][0]
        if not isinstance(column, int):
            column = pl.multiple_of(column, self.unit_columns)
        chunk = self.unit_rows
        while chunk * 2 <= 96 and rows % (chunk * 2) == 0:
            chunk *= 2
        inbox = self.inbox[s]
        array = self.array
        def body(i, carry):
            at = pl.multiple_of(i * chunk, chunk)
            here = (pl.ds(pl.multiple_of(row + at, self.unit_rows), chunk), pl.ds(column, columns))
            array[here] = array[here] + inbox[pl.ds(at, chunk), :]
            return carry
        lax.fori_loop(0, rows // chunk, body, 0)

    def share(self, s):
        if self.plan[s][1] != "full":
            pl.semaphore_wait(self.free.at[s], 1)
            self.share_copy(s).start()

    def collect(self, s):
        if self.plan[s][1] != "full":
            self.share_copy(s).wait()


HIGHEST = lax.Precision.HIGHEST
LANES = 128
PANEL = 2048

def ceil8(v):
    return -(-v // 8) * 8

def sin_cos(x):
    turns = jnp.round(x * (2.0 / math.pi))
    r = ((x - turns * 1.5703125) - turns * 4.837512969970703125e-4) - turns * 7.54978995489188e-8
    quadrant = turns.astype(jnp.int32)
    z = r * r
    s = ((-1.9515295891e-4 * z + 8.3321608736e-3) * z - 1.6666654611e-1) * z * r + r
    c = ((2.443315711809948e-5 * z - 1.388731625493765e-3) * z + 4.166664568298827e-2) * z * z - 0.5 * z + 1.0
    swap = (quadrant & 1) == 1
    sin_part = jnp.where(swap, c, s)
    cos_part = jnp.where(swap, s, c)
    sin_out = jnp.where((quadrant & 2) == 2, -sin_part, sin_part)
    cos_out = jnp.where(((quadrant + 1) & 2) == 2, -cos_part, cos_part)
    return sin_out, cos_out

def dot(a, b, ca, cb, precision=None):
    return lax.dot_general(a, b, (((ca,), (cb,)), ((), ())), precision=precision, preferred_element_type=jnp.float32)

class Sizes:
    def __init__(self, n, rows, local, width, emb, filt, hidden=3072):
        self.hidden, self.block = hidden, hidden // 8
        self.n, self.rows, self.local, self.width, self.emb, self.filt = n, rows, local, width, emb, filt
        self.length = n * local
        self.cpd = width // n
        self.cpad = ceil8(self.cpd)
        self.nb = self.length // LANES
        self.tokens = rows * local
        self.tiles = self.tokens // LANES
        self.erows = ceil8(emb)
        self.panel = min(PANEL, self.length)
        self.panels = self.length // self.panel
        assert local * 2 == LANES and rows == 4

def own_selection(z, me):
    want = lax.broadcasted_iota(jnp.int32, (z.cpad, z.width), 0)
    have = lax.broadcasted_iota(jnp.int32, (z.cpad, z.width), 1)
    return jnp.where((have == want + me * z.cpd) & (want < z.cpd), 1.0, 0.0).astype(jnp.float32)

def embed_rows(z, at, count):
    row = lax.broadcasted_iota(jnp.int32, (z.erows, count), 0)
    t = at + lax.broadcasted_iota(jnp.int32, (z.erows, count), 1)
    bands = (z.emb - 1) // 2
    harmonic = jnp.where(row <= bands, row, row - bands)
    angle = lax.rem(t * harmonic, z.length).astype(jnp.float32) * (2.0 * math.pi / z.length)
    s, c = sin_cos(angle)
    scaled = t.astype(jnp.float32) / z.length
    return jnp.where(row == 0, scaled, jnp.where(row <= bands, c, jnp.where(row < z.emb, s, 0.0)))

def columns(ref, count):
    eye = (lax.broadcasted_iota(jnp.int32, (count, count), 0) == lax.broadcasted_iota(jnp.int32, (count, count), 1)).astype(jnp.float32)
    return dot(eye, jnp.broadcast_to(ref[...], (8, count)), 1, 1, HIGHEST)[:, 0:1]

CHUNK = 512

def filter_setup(z, me, w, keep):
    select = own_selection(z, me)
    keep.own_filter[...] = dot(select, w.filter_weight[...], 1, 1, HIGHEST)
    own_decay = dot(select, jnp.broadcast_to(w.decay_rates[...], (8, z.width)), 1, 1, HIGHEST)[:, 0:1]
    keep.own_decay[...] = jnp.broadcast_to(own_decay, (z.cpad, LANES))
    keep.embed_pad[...] = jnp.zeros((z.erows, z.filt), jnp.float32)
    keep.embed_pad[0:z.emb, :] = w.embed_weight[...]
    keep.bias_one[...] = jnp.broadcast_to(columns(w.embed_bias, z.filt), (z.filt, LANES))
    keep.bias_two[...] = jnp.broadcast_to(columns(w.inner_bias, z.filt), (z.filt, LANES))


def filter_hidden(z, w, keep, at):
    embedded = embed_rows(z, at, CHUNK)
    s1, c1 = sin_cos(dot(keep.embed_pad[...], embedded, 0, 0, HIGHEST) + keep.bias_one[:, 0:1])
    s2, c2 = sin_cos(dot(w.inner_weight[...], s1, 0, 0, HIGHEST) + keep.bias_two[:, 0:1])
    scaled = (at + lax.broadcasted_iota(jnp.int32, (z.cpad, CHUNK), 1)).astype(jnp.float32) / z.length
    window = jnp.exp(-keep.own_decay[:, 0:1] * scaled)
    return embedded, s1, c1, s2, c2, scaled, window


def filter_forward(z, w, keep, begin, end):
    def body(i, carry):
        at = pl.multiple_of(i * CHUNK, CHUNK)
        embedded, s1, c1, s2, c2, scaled, window = filter_hidden(z, w, keep, at)
        keep.taps[:, pl.ds(at, CHUNK)] = dot(keep.own_filter[...], s2, 1, 0, HIGHEST) * window
        return carry
    lax.fori_loop(begin, end, body, 0)

def filter_backward(z, w, keep, grad_taps, sums):
    for ref in vars(sums).values():
        ref[...] = jnp.zeros(ref.shape, jnp.float32)
    def body(i, carry):
        at = pl.multiple_of(i * CHUNK, CHUNK)
        here = (slice(None), pl.ds(at, CHUNK))
        embedded, s1, c1, s2, c2, scaled, window = filter_hidden(z, w, keep, at)
        grad = grad_taps[here]
        decay = -jnp.sum(grad * keep.taps[here] * scaled, axis=1, keepdims=True)
        sums.decay[...] += jnp.broadcast_to(decay, (z.cpad, LANES))
        grad_raw = grad * window
        sums.filter[...] += dot(grad_raw, s2, 1, 1, HIGHEST)
        two = dot(keep.own_filter[...], grad_raw, 0, 0, HIGHEST) * c2
        sums.inner[...] += dot(s1, two, 1, 1, HIGHEST)
        sums.inner_bias[...] += jnp.broadcast_to(jnp.sum(two, axis=1, keepdims=True), (z.filt, LANES))
        one = dot(w.inner_weight[...], two, 1, 0, HIGHEST) * c1
        sums.embed[...] += dot(embedded, one, 1, 1, HIGHEST)
        sums.embed_bias[...] += jnp.broadcast_to(jnp.sum(one, axis=1, keepdims=True), (z.filt, LANES))
        return carry
    lax.fori_loop(0, z.length // CHUNK, body, 0)

def build_toeplitz(z, taps, pool):
    sub = lax.broadcasted_iota(jnp.int32, (8, z.length), 0)
    lane = lax.broadcasted_iota(jnp.int32, (8, LANES), 1)
    sub1 = lax.broadcasted_iota(jnp.int32, (8, LANES), 0)
    def body(c, carry):
        base = jnp.broadcast_to(taps[pl.ds(c, 1), :], (8, z.length))
        for bit in (1, 2, 4):
            base = jnp.where((sub & bit) == bit, pltpu.roll(base, bit, 1), base)
        for q in range(0, LANES // 8, 2):
            parts = []
            for u in (q, q + 1):
                part = pltpu.roll(base, 8 * u, 1) if u else base
                first = jnp.where(lane >= sub1 + 8 * u, part[:, :LANES], 0.0)
                parts.append(jnp.concatenate([first, part[:, LANES:]], axis=1))
            pair = jnp.concatenate(parts, axis=0).astype(jnp.bfloat16)
            for k in range(z.panels):
                at = pl.multiple_of((c * z.panels + k) * LANES, LANES) + 8 * q
                pool[pl.ds(pl.multiple_of(at, 16), 16), :] = pair[:, k * z.panel:(k + 1) * z.panel]
        return carry
    lax.fori_loop(0, z.cpd, body, 0)

def fold_panel(z, k, product, fold):
    lane = lax.broadcasted_iota(jnp.int32, (8, LANES), 1)
    row = lax.broadcasted_iota(jnp.int32, (8, LANES), 0)
    sums, before = None, None
    for u in range(LANES // 8):
        part = product[8 * u:8 * u + 8, :]
        first = part[:, :LANES]
        inside = lane >= row + 8 * u
        part = jnp.concatenate([jnp.where(inside, first, 0.0), part[:, LANES:]], axis=1)
        part = pltpu.roll(part, z.panel - 8 * u, 1) if u else part
        sums = part if sums is None else sums + part
        if k:
            outside = jnp.where(inside, 0.0, first)
            outside = pltpu.roll(outside, LANES - 8 * u, 1) if u else outside
            before = outside if before is None else before + outside
    fold[:, k * z.panel:(k + 1) * z.panel] = sums
    if k:
        fold[:, k * z.panel - LANES:k * z.panel] += before


def fold_rows(z, fold):
    sums = fold[...]
    row = lax.broadcasted_iota(jnp.int32, sums.shape, 0)
    for bit in (1, 2, 4):
        sums = jnp.where((row & bit) == bit, pltpu.roll(sums, z.length - bit, 1), sums)
    return jnp.sum(sums, axis=0, keepdims=True)

class Exchange:
    def __init__(self, outgoing, incoming, sends, arrivals, me, n):
        self.outgoing, self.incoming, self.sends, self.arrivals, self.me, self.n = outgoing, incoming, sends, arrivals, me, n
    def copy(self, k):
        to = lax.rem(self.me + k, self.n)
        return pltpu.make_async_remote_copy(
            src_ref=self.outgoing.at[to], dst_ref=self.incoming.at[self.me],
            send_sem=self.sends.at[k], recv_sem=self.arrivals.at[k],
            device_id=(to,), device_id_type=MESH)
    def start(self):
        def body(k, carry):
            self.copy(k).start()
            return carry
        lax.fori_loop(1, self.n, body, 0)
        self.incoming[self.me] = self.outgoing[self.me]
    def wait(self):
        def body(k, carry):
            self.copy(k).wait()
            return carry
        lax.fori_loop(1, self.n, body, 0)

def each_slab(z, body):
    if z.cpd % 8 == 0:
        lax.fori_loop(0, z.n, body, 0)
    else:
        for k in range(z.n):
            body(k, 0)

def slabs_from_rows(z, flipped, outgoing):
    def body(k, carry):
        at = k * z.cpd
        if z.cpd % 8 == 0:
            at = pl.multiple_of(at, 8)
        slab = flipped[pl.ds(at, z.cpad), :]
        outgoing[k] = jnp.concatenate([slab[:, :LANES], slab[:, LANES:]], axis=0).astype(outgoing.dtype)
        return carry
    each_slab(z, body)

def rows_from_slabs(z, incoming, flipped):
    def body(k, carry):
        at = k * z.cpd
        if z.cpd % 8 == 0:
            at = pl.multiple_of(at, 8)
        slab = incoming[k].astype(jnp.float32)
        flipped[pl.ds(at, z.cpad), :] = jnp.concatenate([slab[:z.cpad], slab[z.cpad:]], axis=1)
        return carry
    each_slab(z, body)

def widen_slabs(z, incoming, wide):
    def body(j, carry):
        wide[pl.ds(pl.multiple_of(j * 2 * z.cpad, 8), 2 * z.cpad), :] = incoming[j].astype(jnp.float32)
        return carry
    lax.fori_loop(0, z.n, body, 0)

def narrow_slabs(z, wide, outgoing):
    def body(j, carry):
        outgoing[j] = wide[pl.ds(pl.multiple_of(j * 2 * z.cpad, 8), 2 * z.cpad), :].astype(outgoing.dtype)
        return carry
    lax.fori_loop(0, z.n, body, 0)

def channel_blocks(z, wide, c):
    lane = lax.broadcasted_iota(jnp.int32, (z.nb, LANES), 1)
    low = lane < LANES // 2
    out = []
    for t in range(2):
        even = wide[pl.ds(t * z.cpad + c, z.nb, 4 * z.cpad), :]
        odd = wide[pl.ds((2 + t) * z.cpad + c, z.nb, 4 * z.cpad), :]
        out.append(jnp.where(low, even, pltpu.roll(odd, LANES // 2, 1)))
        out.append(jnp.where(low, pltpu.roll(even, LANES // 2, 1), odd))
    return out

def put_channel_blocks(z, wide, c, blocks):
    lane = lax.broadcasted_iota(jnp.int32, (z.nb, LANES), 1)
    low = lane < LANES // 2
    for t in range(2):
        a, b = blocks[2 * t], blocks[2 * t + 1]
        wide[pl.ds(t * z.cpad + c, z.nb, 4 * z.cpad), :] = jnp.where(low, a, pltpu.roll(b, LANES // 2, 1))
        wide[pl.ds((2 + t) * z.cpad + c, z.nb, 4 * z.cpad), :] = jnp.where(low, pltpu.roll(a, LANES // 2, 1), b)

def panel_rows(z, c, k):
    return pl.ds(pl.multiple_of((c * z.panels + k) * LANES, LANES), LANES)


def convolve_forward(z, wide, pool, kept, spread):
    each = z.panel // LANES
    def body(c, carry):
        blocks = channel_blocks(z, wide, c)
        x = jnp.concatenate(blocks, axis=0).astype(jnp.bfloat16)
        kept[c] = x
        spread[...] = jnp.zeros(spread.shape, jnp.float32)
        for k in range(z.panels):
            product = dot(x, pool[panel_rows(z, c, k), :], 1, 0)
            for i in range(each):
                d = k * each + i
                for r in range(4):
                    spread[r, d:d + z.nb, :] += product[r * z.nb:(r + 1) * z.nb, i * LANES:(i + 1) * LANES]
        put_channel_blocks(z, wide, c, [spread[r, 0:z.nb, :] for r in range(4)])
        return carry
    lax.fori_loop(0, z.cpd, body, 0)


def convolve_back_channel(z, c, wide, panel_of, kept, spread, advanced, back, fold, grad_taps):
    blocks = channel_blocks(z, wide, c)
    for r in range(4):
        spread[r, 0:z.nb, :] = blocks[r]
    each = z.panel // LANES
    source = kept[c].astype(jnp.float32).T.astype(jnp.bfloat16)
    for k in range(z.panels):
        for i in range(each):
            d = k * each + i
            advanced[:, i * LANES:(i + 1) * LANES] = jnp.concatenate(
                [spread[r, d:d + z.nb, :] for r in range(4)], axis=0).astype(jnp.bfloat16)
        panel = panel_of(c, k)
        product = dot(advanced[...], panel[...], 1, 1)
        back[...] = product if k == 0 else back[...] + product
        fold_panel(z, k, dot(source, advanced[...], 1, 0), fold)
    put_channel_blocks(z, wide, c, [back[r * z.nb:(r + 1) * z.nb, :] for r in range(4)])
    grad_taps[pl.ds(c, 1), :] = fold_rows(z, fold)


class Names:
    def __init__(self, names, values):
        vars(self).update(zip(names, values))


def keep_shapes(z):
    return dict(
        own_filter=(z.cpad, z.filt), own_decay=(z.cpad, LANES), embed_pad=(z.erows, z.filt),
        bias_one=(z.filt, LANES), bias_two=(z.filt, LANES), taps=(z.cpad, z.length),
    )


def sum_shapes(z):
    return dict(
        decay=(z.cpad, LANES), filter=(z.cpad, z.filt), inner=(z.filt, z.filt), inner_bias=(z.filt, LANES),
        embed=(z.erows, z.filt), embed_bias=(z.filt, LANES),
    )


F32, BF16 = jnp.float32, jnp.bfloat16
BLOCKS = 8
WIDE = 256


class Row:
    FIRST_GAIN, FIRST_SHIFT, INPUT_BIAS, SHORT_KERNEL, SHORT_BIAS = 0, 1, 2, 5, 14
    DECAY, FILTER_BIAS, OUTPUT_BIAS, SECOND_GAIN, SECOND_SHIFT, UP_BIAS, DOWN_BIAS = 17, 18, 19, 20, 21, 22, 26
    EMBED_BIAS, INNER_BIAS = 27, 28
    FILTER, NETWORK, TOTAL = 32, 96, 128


def normalize(x):
    center = x - jnp.mean(x, axis=-1, keepdims=True)
    inverse = lax.rsqrt(jnp.mean(center * center, axis=-1, keepdims=True) + EPSILON)
    return center * inverse, inverse


def normalize_back(gradient, gain, unit, inverse):
    q = gradient * gain
    return (q - jnp.mean(q, axis=-1, keepdims=True) - unit * jnp.mean(q * unit, axis=-1, keepdims=True)) * inverse


def as_row(column):
    size = column.shape[0]
    row, lane = (lax.broadcasted_iota(jnp.int32, (size, size), i) for i in range(2))
    return dot(column, jnp.where(row == lane, 1.0, 0.0).astype(F32), 0, 0, HIGHEST)[0:1, :]


def total(x):
    return jnp.sum(x, axis=0, keepdims=True)


def row_masks(z, me, lengths, keep_one, keep_two):
    for r in range(z.rows):
        position = me * z.local + lax.broadcasted_iota(jnp.int32, (z.local, LANES), 0)
        first = position == 0
        second = position == 1
        end = 0
        for j in range(lengths.shape[1] - 1):
            end = end + lengths[r, j]
            first = first | (position == end)
            second = second | (position == end + 1)
        keep_one[r * z.local:(r + 1) * z.local, :] = jnp.where(first, 0.0, 1.0)
        keep_two[r * z.local:(r + 1) * z.local, :] = jnp.where(first | second, 0.0, 1.0)


def lagged(z, values, halo, t, columns):
    row = lax.broadcasted_iota(jnp.int32, (LANES, 1), 0)
    one, two = pltpu.roll(values, 1, 0), pltpu.roll(values, 2, 0)
    for u in range(2):
        r = 2 * t + u
        older, newer = halo[2 * r:2 * r + 1, columns], halo[2 * r + 1:2 * r + 2, columns]
        one = jnp.where(row == u * z.local, newer, one)
        two = jnp.where(row == u * z.local, older, jnp.where(row == u * z.local + 1, newer, two))
    return one, two


def halves(t):
    return slice(t * LANES, (t + 1) * LANES)


class Flow:
    def __init__(self, reduction):
        self.reduction = reduction
        self.steps = len(reduction.plan)
        self.at = -1
    def advance(self):
        s, n, r = self.at, self.steps, self.reduction
        if s < 0:
            r.give(0)
        elif s < n - 1:
            r.take(s)
            r.give(s + 1)
        elif s == n - 1:
            r.take(s)
            r.share(s)
        elif s < 2 * n - 1:
            r.collect(2 * n - 1 - s)
            r.share(2 * n - 2 - s)
        elif s == 2 * n - 1:
            r.collect(0)
        self.at += 1
    @property
    def done(self):
        return self.at >= 2 * self.steps


def block_kernel(z, order, *refs):
    inputs, outs, scratch, fetched, keep_names, sum_names = order
    v = Names(inputs + outs + scratch, refs)
    me = lax.axis_index("seq")
    n = z.n
    d = z.width
    p = Names(fetched, [getattr(v, "v_" + name) for name in fetched])
    def fetch(name):
        source, target = getattr(v, name), getattr(p, name)
        if len(source.shape) == 1:
            target = target.at[0]
        return pltpu.make_async_copy(source, target, v.loads.at[fetched.index(name)])
    late = ("input_weight", "output_weight", "cotangent")
    soon = [name for name in fetched if name not in late]
    for name in soon + list(late):
        fetch(name).start()
    def weight_block(j, slot):
        at = pl.multiple_of(j * z.block, LANES)
        return (
            pltpu.make_async_copy(v.up_weight.at[:, pl.ds(at, z.block)], v.up_slots.at[slot], v.stream.at[0, slot]),
            pltpu.make_async_copy(v.down_weight.at[pl.ds(at, z.block), :], v.down_slots.at[slot], v.stream.at[1, slot]),
        )
    for copy in weight_block(0, 0):
        copy.start()
    barrier = pltpu.get_barrier_semaphore()
    def greet(k, carry):
        pl.semaphore_signal(barrier, inc=1, device_id=(lax.rem(me + k, n),), device_id_type=MESH)
        return carry
    lax.fori_loop(1, n, greet, 0)
    small = v.r_small
    small[0:Row.FILTER, :] = jnp.zeros((Row.FILTER, d), F32)
    small[Row.NETWORK:Row.TOTAL, :] = jnp.zeros((Row.TOTAL - Row.NETWORK, d), F32)
    row_masks(z, me, v.doc_lengths, v.keep_one, v.keep_two)

    for name in soon:
        fetch(name).wait()
    tokens = p.tokens
    for t in range(z.tiles):
        unit, inverse = normalize(tokens[halves(t), :].astype(F32))
        v.unit_one[halves(t), :] = unit
        v.inverse_one[halves(t), :] = jnp.broadcast_to(inverse, (LANES, LANES))
        v.normed[halves(t), :] = (unit * p.first_gain[...] + p.first_shift[...]).astype(BF16)
    fetch("input_weight").wait()
    part = 3 * d // 6
    def project(j, carry):
        here = pl.ds(pl.multiple_of(j * part, LANES), part)
        values = (dot(v.normed[...], p.input_weight[:, here], 1, 0) + p.input_bias[:, here]).astype(BF16)
        v.projected[:, here] = values
        rounded = values.astype(F32)
        for r in range(z.rows):
            last = (r + 1) * z.local
            v.rim_out[2 * r:2 * r + 2, here] = rounded[last - 2:last, :]
        return carry
    lax.fori_loop(0, 6, project, 0)
    pl.semaphore_wait(barrier, n - 1)
    ahead, behind = lax.rem(me + 1, n), lax.rem(me + n - 1, n)
    rim = pltpu.make_async_remote_copy(
        src_ref=v.rim_out, dst_ref=v.rim_in, send_sem=v.rims.at[0], recv_sem=v.rims.at[1],
        device_id=(ahead,), device_id_type=MESH)
    rim.start()
    keep = Names(keep_names, [getattr(v, "k_" + name) for name in keep_names])
    chunks = z.length // CHUNK
    early = chunks // 2
    filter_setup(z, me, p, keep)
    filter_forward(z, p, keep, 0, early)
    rim.wait()

    def short(j, carry):
        inner = pl.ds(pl.multiple_of(j * WIDE, LANES), WIDE)
        for t in range(z.tiles):
            k1, k2 = v.keep_one[halves(t), 0:1], v.keep_two[halves(t), 0:1]
            streams = []
            for s in range(3):
                here = pl.ds(pl.multiple_of(s * d + j * WIDE, LANES), WIDE)
                values = v.projected[halves(t), here].astype(F32)
                one, two = lagged(z, values, v.rim_in, t, here)
                taps = p.short_kernel
                out = (taps[0:1, here] * values + taps[1:2, here] * (k1 * one) + taps[2:3, here] * (k2 * two)
                       + p.short_bias[:, here])
                (v.gate_zero, v.gate_one, v.value_part)[s][halves(t), inner] = out
                streams.append(out)
            v.flipped[inner, halves(t)] = (streams[1] * streams[2]).T
        return carry
    lax.fori_loop(0, d // WIDE, short, 0)
    v.flipped[d:, :] = jnp.zeros((8, z.tokens), F32)

    def exchange(i):
        return Exchange(v.slabs_out.at[i % 2], v.slabs_in.at[i % 2], v.sends.at[i], v.arrivals.at[i], me, n)
    slabs_from_rows(z, v.flipped, v.slabs_out.at[0])
    first = exchange(0)
    first.start()
    filter_forward(z, p, keep, early, chunks)
    build_toeplitz(z, keep.taps, v.pool)
    first.wait()
    widen_slabs(z, v.slabs_in.at[0], v.wide)
    save = pltpu.make_async_copy(v.pool, v.toeplitz_saved, v.saves.at[0])
    save.start()
    convolve_forward(z, v.wide, v.pool, v.kept, v.spread)
    save.wait()
    narrow_slabs(z, v.wide, v.slabs_out.at[1])
    second = exchange(1)
    second.start()
    fetch("output_weight").wait()
    fetch("cotangent").wait()
    cotangent = p.cotangent
    small[Row.DOWN_BIAS:Row.DOWN_BIAS + 1, :] = total(cotangent[...].astype(F32))
    second.wait()
    rows_from_slabs(z, v.slabs_in.at[1], v.flipped)

    def gate(j, carry):
        inner = pl.ds(pl.multiple_of(j * WIDE, LANES), WIDE)
        for t in range(z.tiles):
            gated = v.value_part[halves(t), inner] * v.gate_one[halves(t), inner]
            conv = v.flipped[inner, halves(t)].T + p.filter_bias[:, inner] * gated
            v.conv[halves(t), inner] = conv
            v.mixed[halves(t), inner] = (conv * v.gate_zero[halves(t), inner]).astype(BF16)
        return carry
    lax.fori_loop(0, d // WIDE, gate, 0)
    for t in range(z.tiles):
        branch = dot(v.mixed[halves(t), :], p.output_weight[...], 1, 0) + p.output_bias[...]
        residual = tokens[halves(t), :].astype(F32) + branch
        unit, inverse = normalize(residual)
        v.unit_two[halves(t), :] = unit
        v.inverse_two[halves(t), :] = jnp.broadcast_to(inverse, (LANES, LANES))
        v.normed_two[halves(t), :] = (unit * p.second_gain[...] + p.second_shift[...]).astype(BF16)
        v.residual[halves(t), :] = residual + p.down_bias[...]
    v.grad_normed[...] = jnp.zeros((z.tokens, d), F32)

    arrays = [v.r_down.at[i] for i in range(4)] + [v.r_up.at[i] for i in range(4)] + [v.r_out] + [v.r_inner.at[i] for i in range(3)] + [v.r_small]
    flows = []
    for i, (array, plan) in enumerate(zip(arrays, z.plans)):
        reduction = Reduction(array, plan, part_inboxes(z, v, i), v.part_sends.at[i], v.part_arrivals.at[i], v.part_free.at[i], me)
        flows.append(Flow(reduction))
    def run(parts):
        for i in parts:
            if not flows[i].done:
                flows[i].advance()

    def mlp(j, carry):
        slot = lax.rem(j, 2)
        for copy in weight_block(j, slot):
            copy.wait()
        @pl.when(j + 1 < BLOCKS)
        def _():
            for copy in weight_block(j + 1, 1 - slot):
                copy.start()
        up, down = v.up_slots[slot], v.down_slots[slot]
        here = pl.ds(pl.multiple_of(j * z.block, LANES), z.block)
        x = dot(v.normed_two[...], up, 1, 0) + p.up_bias[:, here]
        grad_hidden = dot(cotangent[...], down, 1, 1)
        root = math.sqrt(2.0 / math.pi)
        square = x * x
        curve = jnp.tanh(root * (x + 0.044715 * (square * x)))
        half = 0.5 * (1.0 + curve)
        hidden = (x * half).astype(BF16)
        slope = half + 0.5 * x * (1.0 - curve * curve) * (root * (1.0 + 3.0 * 0.044715 * square))
        grad_pre = (grad_hidden * slope).astype(BF16)
        v.residual[...] += dot(hidden, down, 1, 0)
        v.grad_normed[...] += dot(grad_pre, up, 1, 1)
        part, half_part = lax.div(j, 2), lax.rem(j, 2)
        there = pl.ds(pl.multiple_of(half_part * z.block, LANES), z.block)
        v.r_down[part, there, :] = dot(hidden, cotangent[...], 0, 0).astype(BF16)
        v.r_up[part, :, there] = dot(v.normed_two[...], grad_pre, 0, 0).astype(BF16)
        v.up_sums[:, here] = total(grad_pre.astype(F32))
        return carry
    for i in range(4):
        lax.fori_loop(2 * i, 2 * i + 2, mlp, 0)
        if i:
            run(Schedule.MLP[i - 1])
        run((i, 4 + i))
    wide_rows = v.up_sums.shape[1] // d
    for i in range(wide_rows):
        small[Row.UP_BIAS + i:Row.UP_BIAS + i + 1, :] = v.up_sums[:, i * d:(i + 1) * d]
    v.output[...] = v.residual[...].astype(BF16)

    gain_sum, shift_sum, bias_sum = 0.0, 0.0, 0.0
    for t in range(z.tiles):
        gradient = v.grad_normed[halves(t), :]
        unit = v.unit_two[halves(t), :]
        gain_sum = gain_sum + total(gradient * unit)
        shift_sum = shift_sum + total(gradient)
        value = cotangent[halves(t), :].astype(F32) + normalize_back(gradient, p.second_gain[...], unit, v.inverse_two[halves(t), 0:1])
        v.residual[halves(t), :] = value
        branch = value.astype(BF16)
        v.grad_branch[halves(t), :] = branch
        bias_sum = bias_sum + total(branch.astype(F32))
    small[Row.SECOND_GAIN:Row.SECOND_GAIN + 1, :] = gain_sum
    small[Row.SECOND_SHIFT:Row.SECOND_SHIFT + 1, :] = shift_sum
    small[Row.OUTPUT_BIAS:Row.OUTPUT_BIAS + 1, :] = bias_sum
    grad_conv, grad_gate_zero = v.unit_two, v.grad_normed
    def mix_back(j, carry):
        inner = pl.ds(pl.multiple_of(j * WIDE, LANES), WIDE)
        sums = jnp.zeros((1, WIDE), F32)
        for t in range(z.tiles):
            grad_mixed = dot(v.grad_branch[halves(t), :], p.output_weight[inner, :], 1, 1)
            back = grad_mixed * v.gate_zero[halves(t), inner]
            grad_conv[halves(t), inner] = back
            grad_gate_zero[halves(t), inner] = grad_mixed * v.conv[halves(t), inner]
            gated = v.value_part[halves(t), inner] * v.gate_one[halves(t), inner]
            sums = sums + total(back * gated)
            v.flipped[inner, halves(t)] = back.T
        small[Row.FILTER_BIAS:Row.FILTER_BIAS + 1, inner] = sums
        return carry
    lax.fori_loop(0, d // WIDE, mix_back, 0)
    slabs_from_rows(z, v.flipped, v.slabs_out.at[0])
    third = exchange(2)
    third.start()
    run(Schedule.THREE)
    def load_panel(i):
        saved = v.toeplitz_saved.at[pl.ds(pl.multiple_of(i * LANES, LANES), LANES), :]
        slot = lax.rem(i, 2)
        return pltpu.make_async_copy(saved, v.toeplitz_slots.at[slot], v.stream.at[2, slot])
    load_panel(0).start()
    def panel_of(c, k):
        i = c * z.panels + k
        load_panel(i).wait()
        @pl.when(i + 1 < z.cpd * z.panels)
        def _():
            load_panel(i + 1).start()
        return v.toeplitz_slots.at[lax.rem(i, 2)]
    def out_grad(j, carry):
        inner = pl.ds(pl.multiple_of(j * WIDE, LANES), WIDE)
        v.r_out[:, inner] = dot(v.mixed[...], v.grad_branch[:, inner], 0, 0).astype(BF16)
        return carry
    lax.fori_loop(0, d // WIDE, out_grad, 0)
    run((8,))
    run(Schedule.WAIT_THREE)
    third.wait()
    widen_slabs(z, v.slabs_in.at[0], v.wide)
    v.spread[...] = jnp.zeros(v.spread.shape, F32)
    v.grad_taps[...] = jnp.zeros(v.grad_taps.shape, F32)
    pieces = len(Schedule.PIECES)
    bounds = [z.cpd * i // pieces for i in range(pieces + 1)]
    def back_channel(c, carry):
        convolve_back_channel(z, c, v.wide, panel_of, v.kept, v.spread, v.advanced, v.back, v.fold, v.grad_taps)
        return carry
    for i in range(pieces):
        lax.fori_loop(bounds[i], bounds[i + 1], back_channel, 0)
        run(Schedule.PIECES[i])
    narrow_slabs(z, v.wide, v.slabs_out.at[1])
    fourth = exchange(3)
    fourth.start()
    run(Schedule.SENT)
    sums = Names(sum_names, [getattr(v, "s_" + name) for name in sum_names])
    filter_backward(z, p, keep, v.grad_taps, sums)
    select = own_selection(z, me)
    small[Row.FILTER:Row.NETWORK, :] = dot(sums.filter[...], select, 0, 0, HIGHEST)
    small[Row.DECAY:Row.DECAY + 1, :] = dot(sums.decay[...], select, 0, 0, HIGHEST)[0:1, :]
    half = z.filt // 2
    small[Row.NETWORK:Row.NETWORK + half, 0:z.filt] = sums.inner[0:half, :]
    small[Row.NETWORK:Row.NETWORK + half, LANES:LANES + z.filt] = sums.inner[half:, :]
    small[Row.NETWORK:Row.NETWORK + half, 2 * LANES:2 * LANES + z.filt] = sums.embed[0:half, :]
    small[Row.NETWORK:Row.NETWORK + z.erows - half, 3 * LANES:3 * LANES + z.filt] = sums.embed[half:, :]
    small[Row.EMBED_BIAS:Row.EMBED_BIAS + 1, 0:z.filt] = as_row(sums.embed_bias[...])
    small[Row.INNER_BIAS:Row.INNER_BIAS + 1, 0:z.filt] = as_row(sums.inner_bias[...])
    run(Schedule.FILTER)
    run(Schedule.WAIT_FOUR)
    fourth.wait()
    rows_from_slabs(z, v.slabs_in.at[1], v.flipped)

    def gate_back(j, carry):
        inner = pl.ds(pl.multiple_of(j * WIDE, LANES), WIDE)
        for t in range(z.tiles):
            grad_gated = v.flipped[inner, halves(t)].T + p.filter_bias[:, inner] * grad_conv[halves(t), inner]
            first_part = grad_gated * v.value_part[halves(t), inner]
            second_part = grad_gated * v.gate_one[halves(t), inner]
            v.gate_one[halves(t), inner] = first_part
            v.value_part[halves(t), inner] = second_part
            for s, value in enumerate((grad_gate_zero[halves(t), inner], first_part, second_part)):
                here = pl.ds(pl.multiple_of(s * d + j * WIDE, LANES), WIDE)
                taps = p.short_kernel
                for u in range(2):
                    r = 2 * t + u
                    lo = u * z.local
                    head = value[lo:lo + 8, :]
                    one = (taps[1:2, here] * v.keep_one[r * z.local:r * z.local + 8, 0:1]) * head
                    two = (taps[2:3, here] * v.keep_two[r * z.local:r * z.local + 8, 0:1]) * head
                    v.rim_back_out[2 * r:2 * r + 1, here] = two[0:1]
                    v.rim_back_out[2 * r + 1:2 * r + 2, here] = one[0:1] + two[1:2]
        return carry
    lax.fori_loop(0, d // WIDE, gate_back, 0)
    rim_back = pltpu.make_async_remote_copy(
        src_ref=v.rim_back_out, dst_ref=v.rim_back_in, send_sem=v.rims.at[2], recv_sem=v.rims.at[3],
        device_id=(behind,), device_id_type=MESH)
    rim_back.start()
    run(Schedule.RIM)
    grad_streams = (grad_gate_zero, v.gate_one, v.value_part)
    def short_sums(j, carry):
        inner = pl.ds(pl.multiple_of(j * WIDE, LANES), WIDE)
        for s in range(3):
            here = pl.ds(pl.multiple_of(s * d + j * WIDE, LANES), WIDE)
            acc = [jnp.zeros((1, WIDE), F32)] * 4
            for t in range(z.tiles):
                k1, k2 = v.keep_one[halves(t), 0:1], v.keep_two[halves(t), 0:1]
                values = v.projected[halves(t), here].astype(F32)
                one, two = lagged(z, values, v.rim_in, t, here)
                value = grad_streams[s][halves(t), inner]
                acc[0] = acc[0] + total(value * values)
                acc[1] = acc[1] + total(value * (k1 * one))
                acc[2] = acc[2] + total(value * (k2 * two))
                acc[3] = acc[3] + total(value)
            for i in range(3):
                small[Row.SHORT_KERNEL + 3 * i + s:Row.SHORT_KERNEL + 3 * i + s + 1, inner] = acc[i]
            small[Row.SHORT_BIAS + s:Row.SHORT_BIAS + s + 1, inner] = acc[3]
        return carry
    lax.fori_loop(0, d // WIDE, short_sums, 0)
    run(Schedule.SHORT)
    rim_back.wait()
    def spread_back(j, carry):
        inner = pl.ds(pl.multiple_of(j * WIDE, LANES), WIDE)
        row = lax.broadcasted_iota(jnp.int32, (LANES, 1), 0)
        for s in range(3):
            here = pl.ds(pl.multiple_of(s * d + j * WIDE, LANES), WIDE)
            taps = p.short_kernel
            sums = jnp.zeros((1, WIDE), F32)
            for t in range(z.tiles):
                k1, k2 = v.keep_one[halves(t), 0:1], v.keep_two[halves(t), 0:1]
                value = grad_streams[s][halves(t), inner]
                one = pltpu.roll((taps[1:2, here] * k1) * value, LANES - 1, 0)
                two = pltpu.roll((taps[2:3, here] * k2) * value, LANES - 2, 0)
                later = one + two
                for u in range(2):
                    r = 2 * t + u
                    last = (u + 1) * z.local - 1
                    far, near = v.rim_back_in[2 * r:2 * r + 1, here], v.rim_back_in[2 * r + 1:2 * r + 2, here]
                    later = jnp.where(row == last, near, jnp.where(row == last - 1, one + far, later))
                low = (taps[0:1, here] * value + later).astype(BF16)
                v.projected[halves(t), here] = low
                sums = sums + total(low.astype(F32))
            small[Row.INPUT_BIAS + s:Row.INPUT_BIAS + s + 1, inner] = sums
        return carry
    lax.fori_loop(0, d // WIDE, spread_back, 0)
    run(Schedule.SPREAD)
    for k in range(3):
        v.r_inner[k] = dot(v.normed[...], v.projected[:, k * d:(k + 1) * d], 0, 0).astype(BF16)
        run((9 + k,))
    run(Schedule.NORMAL)
    v.conv[...] = jnp.zeros((z.tokens, d), F32)
    def norm_grad(j, carry):
        here = pl.ds(pl.multiple_of(j * part, LANES), part)
        v.conv[...] += dot(v.projected[:, here], p.input_weight[:, here], 1, 1)
        return carry
    lax.fori_loop(0, 6, norm_grad, 0)
    gain_sum, shift_sum = 0.0, 0.0
    for t in range(z.tiles):
        gradient = v.conv[halves(t), :]
        unit = v.unit_one[halves(t), :]
        gain_sum = gain_sum + total(gradient * unit)
        shift_sum = shift_sum + total(gradient)
        value = v.residual[halves(t), :] + normalize_back(gradient, p.first_gain[...], unit, v.inverse_one[halves(t), 0:1])
        v.grad_tokens[halves(t), :] = value.astype(BF16)
    small[Row.FIRST_GAIN:Row.FIRST_GAIN + 1, :] = gain_sum
    small[Row.FIRST_SHIFT:Row.FIRST_SHIFT + 1, :] = shift_sum
    run((12,))

    run(Schedule.TAIL)
    while not all(flow.done for flow in flows):
        run(range(len(flows)))


class Schedule:
    ORDERS = (
        (0, 1, 2, 3, 4),
        (0, 2, 1, 3, 4),
        (0, 2, 3, 1, 4),
        (0, 2, 1, 3, 4),
        (0, 2, 1, 3, 4),
        (0, 3, 2, 1, 4),
        (0, 1, 2, 3, 4),
        (0, 1, 2, 3, 4),
        (0, 3, 1, 2, 4),
        (0, 2, 1, 3, 4),
        (0, 1, 3, 2, 4),
        (0, 3, 2, 1, 4),
        (0, 2, 1, 3, 4),
    )
    MLP = (
        (0, 4,),
        (),
        (),
    )
    THREE = (1, 5, 2, 6, 0, 4, 3, 7,)
    WAIT_THREE = (8,)
    SENT = (3, 2, 6, 1, 7, 5, 0, 8, 4,)
    FILTER = ()
    WAIT_FOUR = ()
    RIM = (3, 4, 7, 2, 0, 6,)
    SHORT = (1, 5, 2, 8,)
    SPREAD = ()
    NORMAL = (9, 1, 4,)
    TAIL = (
        10, 11, 2, 4, 3, 0, 12, 9, 10, 11, 7, 2, 12, 10, 6, 2, 0, 3, 11, 8, 7, 0, 9, 10,
        1, 12, 5, 6, 11, 3, 9, 8, 12, 10, 11, 7, 1, 9, 12, 10, 1, 6, 11, 9, 12, 5, 10, 3,
        9, 12, 8, 6, 11, 10, 5, 6, 9, 12, 7, 3, 8, 3, 11, 8, 10, 5, 10, 9, 5, 12, 9, 7,
        12, 11, 7, 11,
    )
    PIECES = (
        (1, 6,),
        (5, 4,),
        (2,),
        (8, 0, 4, 7,),
        (2, 1, 0,),
        (3, 4, 8, 2, 1, 6,),
        (0, 4, 5,),
        (),
    )


def part_shapes(z):
    d = z.width
    return dict(down=((4, d, d), BF16), up=((4, d, d), BF16), out=((d, d), BF16), inner=((3, d, d), BF16), small=((Row.TOTAL, d), F32))


def part_plans(z):
    bits = [1 << i for i in range(z.n.bit_length() - 1)]
    plans = []
    for i, order in enumerate(Schedule.ORDERS):
        ordered = [bits[k] for k in order] + bits[len(order):] if len(bits) >= len(order) else bits
        rows = Row.TOTAL if i == len(Schedule.ORDERS) - 1 else z.width
        plans.append(halving_plan(rows, z.width, ordered, 8))
    return plans


def part_inboxes(z, v, i):
    d = z.width
    if i < 8:
        box = v.pool.at[pl.ds((i // 2) * d, d), pl.ds((i % 2) * d, d)]
    elif i < 12:
        box = v.boxes.at[i - 8]
    else:
        box = v.small_box
    views, row, column = [], 0, 0
    for _, _, rows, columns in z.plans[i]:
        views.append(box.at[pl.ds(row, rows), pl.ds(column, columns)])
        if columns == d:
            row += rows
        else:
            column += columns
            if column == d:
                row, column = row + rows, 0
    return views


def block(z, inputs, collective_id=0):
    d, f = z.width, z.hidden
    shapes = part_shapes(z)
    keep = keep_shapes(z)
    sums = sum_shapes(z)
    names, specs = [], []
    any_space = pl.BlockSpec(memory_space=pl.ANY)
    for name in inputs:
        names.append(name)
        specs.append(pl.BlockSpec(memory_space=pltpu.SMEM) if name == "doc_lengths" else any_space)
    outs = dict(output=((z.tokens, d), BF16), grad_tokens=((z.tokens, d), BF16))
    for name in shapes:
        outs["r_" + name] = shapes[name]
    pool = (z.cpd * z.panels * LANES, z.panel)
    saved = "toeplitz_saved"
    outs[saved] = (pool, BF16)
    scratch = {}
    fetched = tuple(name for name in inputs if name not in ("doc_lengths", "up_weight", "down_weight"))
    for name in fetched:
        shape = inputs[name].shape
        scratch["v_" + name] = pltpu.VMEM(shape if len(shape) > 1 else (1,) + shape, inputs[name].dtype)
    t = z.tokens
    buffers = dict(
        unit_one=((t, d), F32), inverse_one=((t, LANES), F32), normed=((t, d), BF16), projected=((t, 3 * d), BF16),
        rim_out=((8, 3 * d), F32), rim_in=((8, 3 * d), F32), rim_back_out=((8, 3 * d), F32), rim_back_in=((8, 3 * d), F32),
        keep_one=((t, LANES), F32), keep_two=((t, LANES), F32),
        gate_zero=((t, d), F32), gate_one=((t, d), F32), value_part=((t, d), F32),
        flipped=((d + 8, t), F32), slabs_out=((2, z.n, 2 * z.cpad, LANES), BF16), slabs_in=((2, z.n, 2 * z.cpad, LANES), BF16),
        wide=((z.n * 2 * z.cpad, LANES), F32), spread=((4, 2 * z.nb, LANES), F32), kept=((z.cpd, 4 * z.nb, LANES), BF16),
        pool=(pool, BF16),
        conv=((t, d), F32), mixed=((t, d), BF16), unit_two=((t, d), F32), inverse_two=((t, LANES), F32),
        normed_two=((t, d), BF16), residual=((t, d), F32), grad_normed=((t, d), F32),
        up_slots=((2, d, z.block), BF16), down_slots=((2, z.block, d), BF16), up_sums=((1, f), F32),
        grad_branch=((t, d), BF16), toeplitz_slots=((2, LANES, z.panel), BF16), back=((4 * z.nb, LANES), F32), fold=((8, z.length), F32),
        advanced=((4 * z.nb, z.panel), BF16), grad_taps=((z.cpad, z.length), F32),
    )
    for name, (shape, kind) in buffers.items():
        scratch[name] = pltpu.VMEM(shape, kind)
    for name in keep:
        scratch["k_" + name] = pltpu.VMEM(keep[name], F32)
    for name in sums:
        scratch["s_" + name] = pltpu.VMEM(sums[name], F32)
    steps, count = len(z.plans[0]), len(z.plans)
    scratch.update(
        boxes=pltpu.VMEM((4, d, d), BF16), small_box=pltpu.VMEM((Row.TOTAL + 8, d), F32),
        part_sends=pltpu.SemaphoreType.DMA((count, 2 * steps)), part_arrivals=pltpu.SemaphoreType.DMA((count, 2 * steps)),
        part_free=pltpu.SemaphoreType.REGULAR((count, steps)),
        loads=pltpu.SemaphoreType.DMA((len(fetched),)), stream=pltpu.SemaphoreType.DMA((3, 2)),
        saves=pltpu.SemaphoreType.DMA((1,)), rims=pltpu.SemaphoreType.DMA((4,)),
        sends=pltpu.SemaphoreType.DMA((4, z.n)), arrivals=pltpu.SemaphoreType.DMA((4, z.n)),
    )
    order = (tuple(names), tuple(outs), tuple(scratch), fetched, tuple(keep), tuple(sums))
    results = pl.pallas_call(
        functools.partial(block_kernel, z, order),
        out_shape=[jax.ShapeDtypeStruct(*outs[name]) if name == saved else pltpu.VMEM(*outs[name]) for name in outs],
        in_specs=specs,
        out_specs=[any_space if name == saved else pl.BlockSpec(memory_space=pltpu.VMEM) for name in outs],
        scratch_shapes=list(scratch.values()),
        compiler_params=pltpu.CompilerParams(collective_id=collective_id, has_side_effects=True, vmem_limit_bytes=47 << 20),
        name="hyena_block",
    )(*inputs.values())
    return dict(zip(outs, results))


def finish_layout(z):
    d, f = z.width, z.hidden
    return dict(
        grad_down_weight=((f, d), [("down", i, i * d, 0) for i in range(4)]),
        grad_up_weight=((d, f), [("up", i, 0, i * d) for i in range(4)]),
        grad_output_weight=((d, d), [("out", None, 0, 0)]),
        grad_input_weight=((d, 3 * d), [("inner", i, 0, i * d) for i in range(3)]),
    )


def small_layout(z):
    d, half = z.width, z.filt // 2
    def line(row, count=1):
        return (count * d,), [(row + i, 0, 1, d, 0, i * d) for i in range(count)]
    def short(row):
        return (z.filt,), [(row, 0, 1, z.filt, 0, 0)]
    return dict(
        grad_first_gain=line(Row.FIRST_GAIN), grad_first_shift=line(Row.FIRST_SHIFT), grad_input_bias=line(Row.INPUT_BIAS, 3),
        grad_short_kernel=((3, 3 * d), [(Row.SHORT_KERNEL + 3 * i + s, 0, 1, d, i, s * d) for i in range(3) for s in range(3)]),
        grad_short_bias=line(Row.SHORT_BIAS, 3),
        grad_embed_weight=((z.emb, z.filt), [
            (Row.NETWORK, 2 * LANES, half, z.filt, 0, 0), (Row.NETWORK, 3 * LANES, z.emb - half, z.filt, half, 0)]),
        grad_embed_bias=short(Row.EMBED_BIAS),
        grad_inner_weight=((z.filt, z.filt), [
            (Row.NETWORK, 0, half, z.filt, 0, 0), (Row.NETWORK, LANES, half, z.filt, half, 0)]),
        grad_inner_bias=short(Row.INNER_BIAS),
        grad_filter_weight=((z.filt, d), [(Row.FILTER, 0, z.filt, d, 0, 0)]),
        grad_decay_rates=line(Row.DECAY), grad_filter_bias=line(Row.FILTER_BIAS), grad_output_bias=line(Row.OUTPUT_BIAS),
        grad_second_gain=line(Row.SECOND_GAIN), grad_second_shift=line(Row.SECOND_SHIFT),
        grad_up_bias=line(Row.UP_BIAS, z.hidden // d), grad_down_bias=line(Row.DOWN_BIAS),
    )


RUN = 384


def finish_kernel(z, order, pieces, *refs):
    weights, little, names = order
    v = Names(names, refs)
    stores = []
    landed = []
    for i, (part, index, name, row, column, at, rows, columns) in enumerate(pieces):
        source = getattr(v, "r_" + part)
        landed.append(source if index is None else source.at[index])
        wide, out = getattr(v, "w_" + name), getattr(v, name)
        there = (pl.ds(row, rows), pl.ds(column, columns))
        stores.append(pltpu.make_async_copy(wide.at[there], out.at[there], v.stores.at[i]))
    others = [
        pltpu.make_async_copy(v.block_output, v.output, v.others.at[0]),
        pltpu.make_async_copy(v.block_grad_tokens, v.grad_tokens, v.others.at[1]),
    ]
    for copy in others:
        copy.start()
    for i, (part, index, name, row, column, at, rows, columns) in enumerate(pieces):
        getattr(v, "w_" + name)[row:row + rows, column:column + columns] = landed[i][at:at + rows, :].astype(F32)
        stores[i].start()
    for name, (shape, moves) in small_layout(z).items():
        out = getattr(v, name)
        for row, column, rows, columns, to_row, to_column in moves:
            value = v.r_small[row:row + rows, column:column + columns]
            if len(shape) == 1:
                out[to_column:to_column + columns] = value.reshape(columns)
            else:
                out[to_row:to_row + rows, to_column:to_column + columns] = value
    for copy in stores + others:
        copy.wait()


def finish(z, results):
    layout, little = finish_layout(z), small_layout(z)
    shapes = part_shapes(z)
    pieces = []
    for name in layout:
        for part, index, row, column in layout[name][1]:
            rows, columns = shapes[part][0][-2:]
            for at in range(0, rows, RUN):
                pieces.append((part, index, name, row + at, column, at, min(RUN, rows - at), columns))
    any_space, vmem = pl.BlockSpec(memory_space=pl.ANY), pl.BlockSpec(memory_space=pltpu.VMEM)
    arguments = dict(("r_" + part, results["r_" + part]) for part in shapes)
    arguments.update(block_output=results["output"], block_grad_tokens=results["grad_tokens"])
    arguments = dict((name, pltpu.with_memory_space_constraint(value, pltpu.VMEM)) for name, value in arguments.items())
    outs = dict((name, jax.ShapeDtypeStruct(layout[name][0], F32)) for name in layout)
    token_shape = jax.ShapeDtypeStruct((z.tokens, z.width), BF16)
    outs.update(output=token_shape, grad_tokens=token_shape)
    outs.update((name, jax.ShapeDtypeStruct(little[name][0], F32)) for name in little)
    scratch = dict(("w_" + name, pltpu.VMEM(layout[name][0], F32)) for name in layout)
    scratch.update(
        stores=pltpu.SemaphoreType.DMA((len(pieces),)), others=pltpu.SemaphoreType.DMA((2,))
    )
    names = tuple(arguments) + tuple(outs) + tuple(scratch)
    outputs = pl.pallas_call(
        functools.partial(finish_kernel, z, (tuple(layout), tuple(little), names), pieces),
        out_shape=list(outs.values()),
        in_specs=[vmem] * len(arguments),
        out_specs=[any_space] * (len(layout) + 2) + [vmem] * len(little),
        scratch_shapes=list(scratch.values()),
        compiler_params=pltpu.CompilerParams(vmem_limit_bytes=30 << 20),
        name="widen_gradients",
    )(*arguments.values())
    return Names(outs, outputs)


def shards(
    n, tokens, doc_lengths, first_gain, first_shift, input_weight, input_bias, short_kernel, short_bias, embed_weight, embed_bias,
    inner_weight, inner_bias, filter_weight, decay_rates, filter_bias, output_weight, output_bias, second_gain, second_shift,
    up_weight, up_bias, down_weight, down_bias, cotangent,
):
    rows, local, width = tokens.shape
    z = Sizes(n, rows, local, width, *embed_weight.shape, up_weight.shape[1])
    z.plans = part_plans(z)
    inputs = dict(
        tokens=tokens.reshape(rows * local, width), doc_lengths=doc_lengths, first_gain=first_gain, first_shift=first_shift,
        input_weight=input_weight, input_bias=input_bias, short_kernel=short_kernel, short_bias=short_bias, embed_weight=embed_weight,
        embed_bias=embed_bias, inner_weight=inner_weight, inner_bias=inner_bias, filter_weight=filter_weight, decay_rates=decay_rates,
        filter_bias=filter_bias, output_weight=output_weight, output_bias=output_bias, second_gain=second_gain,
        second_shift=second_shift, up_weight=up_weight, up_bias=up_bias, down_weight=down_weight, down_bias=down_bias,
        cotangent=cotangent.reshape(rows * local, width),
    )
    o = finish(z, block(z, inputs))
    return (
        o.output.reshape(tokens.shape), o.grad_tokens.reshape(tokens.shape), o.grad_first_gain, o.grad_first_shift, o.grad_input_weight,
        o.grad_input_bias, o.grad_short_kernel, o.grad_short_bias, o.grad_embed_weight, o.grad_embed_bias, o.grad_inner_weight,
        o.grad_inner_bias, o.grad_filter_weight, o.grad_decay_rates, o.grad_filter_bias, o.grad_output_weight, o.grad_output_bias,
        o.grad_second_gain, o.grad_second_shift, o.grad_up_weight, o.grad_up_bias, o.grad_down_weight, o.grad_down_bias,
    )


def solution(mesh):
    split, whole = P(None, "seq", None), P()
    return jax.shard_map(
        functools.partial(shards, mesh.shape["seq"]),
        mesh=mesh,
        in_specs=(split,) + (whole,) * 22 + (split,),
        out_specs=(split, split) + (whole,) * 21,
        check_vma=False,
    )
```

profile of v0, /device:TPU:0, one launch (start us, length us, event | category | flops | bytes accessed | tf_op | source)
XLA Modules:
  0.0 207.8 jit_solution(12831977812415517146)
XLA Ops:
  0.7 196.3 %hyena_block.1 = (bf16[256,768]{1,0:T(8,128)(2,1)S(1)}, bf16[256,768]{1,0:T(8,128)(2,1)S(1)}, bf16[4,768,768]{2,1,0:T(8,128)(2,1)S(1)}, bf16[4,768,768]{2,1,0:T(...) custom-call(bf16[256,768]{1,0:T(8,128)(2,1)} %bitcast.4, ...), custom_call_target="tpu_custom_call" | custom-call | tf_op jit(solution)/shard_map/hyena_block/pallas_call | solution.py:995
  197.0 10.6 %widen_gradients.1 = (f32[3072,768]{1,0:T(8,128)}, f32[768,3072]{1,0:T(8,128)}, f32[768,768]{1,0:T(8,128)}, f32[768,2304]{1,0:T(8,128)}, bf16[256,768]{1,0:T(8,1...) custom-call(bf16[4,768,768]{2,1,0:T(8,128)(2,1)S(1)} %get-tuple-elem, ...), custom_call_target="tpu_custom_call" | custom-call | tf_op jit(solution)/shard_map/widen_gradients/pallas_call | solution.py:1097
where the time goes:
time: 209 us; the launch traced here: 208 us
  Pallas kernels  207 us (99%)
    pallas_call x1, Pallas kernels, block(): pl.pallas_call(functools.partial(block_kernel, z, order), out_shape=[jax....  196 us
    pallas_call x1, Pallas kernels, finish(): pl.pallas_call(functools.partial(finish_kernel, z, (tuple(layout), tuple(...  10.6 us

commit v1 on v0

--- a/solution.py
+++ b/solution.py
@@ -859,48 +859,48 @@
 
 class Schedule:
     ORDERS = (
-        (0, 1, 2, 3, 4),
-        (0, 2, 1, 3, 4),
-        (0, 2, 3, 1, 4),
-        (0, 2, 1, 3, 4),
-        (0, 2, 1, 3, 4),
-        (0, 3, 2, 1, 4),
-        (0, 1, 2, 3, 4),
-        (0, 1, 2, 3, 4),
         (0, 3, 1, 2, 4),
         (0, 2, 1, 3, 4),
         (0, 1, 3, 2, 4),
+        (0, 2, 1, 3, 4),
+        (0, 2, 1, 3, 4),
+        (0, 1, 3, 2, 4),
+        (0, 3, 1, 2, 4),
+        (0, 1, 2, 3, 4),
+        (0, 1, 3, 2, 4),
         (0, 3, 2, 1, 4),
+        (0, 2, 1, 3, 4),
+        (0, 1, 2, 3, 4),
         (0, 2, 1, 3, 4),
     )
     MLP = (
         (0, 4,),
         (),
+        (5,),
+    )
+    THREE = (1, 2, 6, 0, 4, 3, 7, 5,)
+    WAIT_THREE = (8,)
+    SENT = (7, 0, 5, 1, 4, 2, 6, 8,)
+    FILTER = (7, 3, 0,)
+    WAIT_FOUR = (5, 1, 2,)
+    RIM = (6, 4, 0, 8, 7, 3,)
+    SHORT = (5, 4, 1, 2,)
+    SPREAD = ()
+    NORMAL = (9, 5, 4,)
+    TAIL = (
+        10, 11, 0, 5, 4, 2, 12, 0, 6, 2, 8, 9, 10, 7, 11, 3, 12, 6, 1, 10, 9, 8, 3, 12,
+        1, 10, 11, 9, 7, 3, 6, 12, 1, 10, 11, 9, 7, 12, 3, 10, 11, 9, 12, 10, 8, 1, 11, 12,
+        6, 1, 7, 9, 8, 7, 11, 3, 10, 3, 12, 9, 6, 11, 6, 8, 8, 9, 10, 9, 12, 11, 10, 12,
+        11,
+    )
+    PIECES = (
+        (1, 2,),
+        (6, 0,),
+        (5, 3, 4, 0, 2,),
+        (5, 4,),
+        (7, 2, 0, 5,),
+        (4, 2, 8,),
         (),
-    )
-    THREE = (1, 5, 2, 6, 0, 4, 3, 7,)
-    WAIT_THREE = (8,)
-    SENT = (3, 2, 6, 1, 7, 5, 0, 8, 4,)
-    FILTER = ()
-    WAIT_FOUR = ()
-    RIM = (3, 4, 7, 2, 0, 6,)
-    SHORT = (1, 5, 2, 8,)
-    SPREAD = ()
-    NORMAL = (9, 1, 4,)
-    TAIL = (
-        10, 11, 2, 4, 3, 0, 12, 9, 10, 11, 7, 2, 12, 10, 6, 2, 0, 3, 11, 8, 7, 0, 9, 10,
-        1, 12, 5, 6, 11, 3, 9, 8, 12, 10, 11, 7, 1, 9, 12, 10, 1, 6, 11, 9, 12, 5, 10, 3,
-        9, 12, 8, 6, 11, 10, 5, 6, 9, 12, 7, 3, 8, 3, 11, 8, 10, 5, 10, 9, 5, 12, 9, 7,
-        12, 11, 7, 11,
-    )
-    PIECES = (
-        (1, 6,),
-        (5, 4,),
-        (2,),
-        (8, 0, 4, 7,),
-        (2, 1, 0,),
-        (3, 4, 8, 2, 1, 6,),
-        (0, 4, 5,),
         (),
     )
 

time: 209 us -> 211 us (level)
    pallas_call x1, Pallas kernels: 196 us -> 199 us  [block(): pl.pallas_call(functools.partial(block_kernel, z, order), out_shape=[jax....]
where the time goes in v1:
time: 211 us; the launch traced here: 210 us
  Pallas kernels  209 us (99%)
    pallas_call x1, Pallas kernels, block(): pl.pallas_call(functools.partial(block_kernel, z, order), out_shape=[jax....  199 us
    pallas_call x1, Pallas kernels, finish(): pl.pallas_call(functools.partial(finish_kernel, z, (tuple(layout), tuple(...  10.6 us

profile of v1, /device:TPU:0, one launch (start us, length us, event | category | flops | bytes accessed | tf_op | source)
XLA Modules:
  0.0 210.0 jit_solution(13024049961342022968)
XLA Ops:
  0.7 198.6 %hyena_block.1 = (bf16[256,768]{1,0:T(8,128)(2,1)S(1)}, bf16[256,768]{1,0:T(8,128)(2,1)S(1)}, bf16[4,768,768]{2,1,0:T(8,128)(2,1)S(1)}, bf16[4,768,768]{2,1,0:T(...) custom-call(bf16[256,768]{1,0:T(8,128)(2,1)} %bitcast.4, ...), custom_call_target="tpu_custom_call" | custom-call | tf_op jit(solution)/shard_map/hyena_block/pallas_call | solution.py:995
  199.2 10.6 %widen_gradients.1 = (f32[3072,768]{1,0:T(8,128)}, f32[768,3072]{1,0:T(8,128)}, f32[768,768]{1,0:T(8,128)}, f32[768,2304]{1,0:T(8,128)}, bf16[256,768]{1,0:T(8,1...) custom-call(bf16[4,768,768]{2,1,0:T(8,128)(2,1)S(1)} %get-tuple-elem, ...), custom_call_target="tpu_custom_call" | custom-call | tf_op jit(solution)/shard_map/widen_gradients/pallas_call | solution.py:1097
